TPU v7x, 32 devices: a whole 2x2x4 slice. The times are simulated.
32 devices in a mesh: section: 4 (over x, core), expert: 4 (over z), tensor: 2 (over y).
Axes of the slice: x: 2, y: 2, z: 4, core: 2. Of those that a mesh axis runs over, the one named last changes fastest.
Arguments:
- tokens: bfloat16 [2048, 5120], P(('section', 'expert'), 'tensor'), may hold values from -6 to 6
- norm_gain: float32 [5120], P('tensor'), may hold values from 0.1 to 1.9
- router: bfloat16 [5120, 4], P('tensor'), may hold values from -0.078125 to 0.078125
- expert_ids: int32 [2048, 1], P(('section', 'expert')), may hold values from 0 to 3; in each aligned block of 128 rows (0 to 127, 128 to 255, ...) at most 64 rows name the same one
- gate_proj: bfloat16 [4, 5120, 4096], P('expert', None, ('section', 'tensor')), may hold values from -0.078125 to 0.078125
- up_proj: bfloat16 [4, 5120, 4096], P('expert', None, ('section', 'tensor')), may hold values from -0.078125 to 0.078125
- down_proj: bfloat16 [4, 4096, 5120], P('expert', 'section', 'tensor'), may hold values from -0.09375 to 0.09375
Outputs:
- moe_out: bfloat16 [2048, 5120], P(('section', 'expert'), 'tensor')
Inputs may be any that keep to these rules, and one draw needn't show every extreme that they name: `expert_ids`: within each aligned block of 128 tokens (the tokens of one group of devices along section and expert) no expert is named by more than 64 tokens, a bound that some block reaches.
All inputs are finite; a program needn't handle non-finite values.
Results may differ from a plain program's by a relative error of at most 0.017.
Values may be sent and summed in bfloat16 or wider, within the bound.
A program may use at most 64 MiB of HBM per device.

v0:
```python
import jax
import jax.numpy as jnp
from jax import lax
from jax.sharding import PartitionSpec as P

D = 5120
EPSILON = 1e-05


def slot_table(expert_ids, experts, capacity):
    chosen = expert_ids[:, 0]
    member = (chosen[:, None] == jnp.arange(experts, dtype=jnp.int32)[None, :]).astype(jnp.int32)
    earlier = jnp.cumsum(member, axis=0) - member
    placed = chosen * capacity + jnp.sum(earlier * member, axis=1)
    placing = placed[:, None] == jnp.arange(experts * capacity, dtype=jnp.int32)[None, :]
    return (member, placing)


def normalize(tokens, norm_gain, squares):
    values = tokens.astype(jnp.float32)
    return (values * lax.rsqrt(squares / D + EPSILON) * norm_gain).astype(jnp.bfloat16)


def on_device(tokens, norm_gain, router, expert_ids, gate_proj, up_proj, down_proj):
    row_count = tokens.shape[0]
    experts = router.shape[1]
    capacity = 2 * row_count // experts
    values = tokens.astype(jnp.float32)
    squares = lax.psum(jnp.sum(values * values, axis=1, keepdims=True), "tensor")
    normed = normalize(tokens, norm_gain, squares)
    logits = lax.psum(jnp.dot(normed, router, preferred_element_type=jnp.float32), "tensor")
    member, placing = slot_table(expert_ids, experts, capacity)
    score = jax.nn.sigmoid(jnp.sum(jnp.where(member > 0, logits, jnp.float32(0.0)), axis=1))
    routed = (normed.astype(jnp.float32) * score[:, None]).astype(jnp.bfloat16)
    placing = placing.astype(jnp.bfloat16)
    outgoing = jnp.einsum("tc,td->cd", placing, routed, preferred_element_type=jnp.float32).astype(
        jnp.bfloat16
    )
    arrived = lax.all_to_all(outgoing, "expert", split_axis=0, concat_axis=0, tiled=True)
    gate_cols = gate_proj[0]
    up_cols = up_proj[0]
    down_rows = down_proj[0]
    widened = lax.all_gather(arrived, "tensor", axis=1, tiled=True)
    piece = lax.all_gather(widened, "section", axis=0, tiled=True)
    gate = jnp.dot(piece, gate_cols, preferred_element_type=jnp.float32)
    upper = jnp.dot(piece, up_cols, preferred_element_type=jnp.float32)
    hidden = (jax.nn.silu(gate) * upper).astype(jnp.bfloat16)
    full_hidden = lax.all_gather(hidden, "tensor", axis=1, tiled=True)
    summed = lax.psum_scatter(
        jnp.dot(full_hidden, down_rows, preferred_element_type=jnp.float32),
        "section",
        scatter_dimension=0,
        tiled=True,
    )
    returned = lax.all_to_all(
        summed.astype(jnp.bfloat16), "expert", split_axis=0, concat_axis=0, tiled=True
    )
    result = jnp.einsum("tc,cd->td", placing, returned, preferred_element_type=jnp.float32)
    return result.astype(jnp.bfloat16)


def solution(mesh):
    in_specs = (
        P(("section", "expert"), "tensor"),
        P("tensor"),
        P("tensor", None),
        P(("section", "expert"), None),
        P("expert", None, ("section", "tensor")),
        P("expert", None, ("section", "tensor")),
        P("expert", "section", "tensor"),
    )
    out_specs = P(("section", "expert"), "tensor")
    return jax.shard_map(
        on_device, mesh=mesh, in_specs=in_specs, out_specs=out_specs, check_vma=False
    )
```

profile of v0, /device:TPU:0, one launch (start us, length us, event | category | flops | bytes accessed | tf_op | source)
XLA Modules:
  0.0 360.6 jit_solution(11621119919947402343)
XLA Ops:
  6.5 0.0 copy-start
  6.5 0.0 copy-start.1
  6.5 0.0 copy-start.2
  6.5 0.0 copy-start.3
  6.5 0.0 all-gather.4.cloned.1.call-start
  6.6 1.4 fusion.8
  7.9 5.9 %psum.14 = f32[128,1]{0,1:T(1,128)S(1)} all-reduce(f32[128,1]{0,1:T(1,128)S(1)} %bitcast.37), channel_id=1, replica_groups=mesh['section'=4,'expert'=4,'tensor'=2] {'tensor'}, use_global_device_ids=true, to_apply=%region_3.0 | all-reduce | flops 128 | bytes 1024 | tf_op jit(solution)/shard_map/psum | solution.py:29
  13.8 0.0 copy-done
  13.9 1.5 fusion.12
  15.3 9.4 %psum.15 = f32[128,4]{1,0:T(8,128)S(1)} all-reduce(f32[128,4]{1,0:T(8,128)S(1)} %fusion.12), channel_id=1, replica_groups=mesh['section'=4,'expert'=4,'tensor'=2] {'tensor'}, use_global_device_ids=true, to_apply=%region_4.5 | all-reduce | flops 512 | bytes 4096 | tf_op jit(solution)/shard_map/psum | solution.py:31
  24.7 0.0 copy-done.3
  24.7 0.1 fusion.17
  24.8 0.2 select_reduce_fusion
  25.0 0.2 reduce_window_sum.11
  25.2 0.2 select_reduce_fusion.1
  25.4 0.0 copy-done.1
  25.4 0.0 copy-done.2
  25.4 0.6 convolution_convert_fusion
  26.0 33.1 %all_to_all.24 = bf16[4,64,2560]{2,1,0:T(8,128)(2,1)} all-to-all(bf16[4,64,2560]{2,1,0:T(8,128)(2,1)S(1)} %bitcast.31), channel_id=1, replica_groups=mesh['section'=4,'expert'=4,'tensor'=2] {'expert'}, dimensions={0} | all-to-all | bytes 2621440 | tf_op jit(solution)/shard_map/all_to_all | solution.py:39
  59.1 0.0 all-gather.4.cloned.1.call-update
  59.2 0.0 all-gather.6.cloned.1.call-start
  59.2 37.2 %all-gather.4.cloned.1.call-done = bf16[256,5120]{1,0:T(8,128)(2,1)} async-done(((bf16[256,2560]{1,0:T(8,128)(2,1)}), bf16[256,5120]{1,0:T(8,128)(2,1)}) %all-gather.4.cloned.1.call-update) | async-done | bytes 2621456 | tf_op jit(solution)/shard_map/all_gather | solution.py:43
  96.5 0.0 all-gather.6.cloned.1.call-update
  96.5 0.0 all-gather.8.cloned.1.call-start
  96.5 71.7 %all-gather.6.cloned.1.call-done = bf16[1024,5120]{1,0:T(8,128)(2,1)} async-done(((bf16[256,5120]{1,0:T(8,128)(2,1)}), bf16[1024,5120]{1,0:T(8,128)(2,1)}) %all-gather.6.cloned.1.call-update) | async-done | bytes 10485776 | tf_op jit(solution)/shard_map/all_gather | solution.py:44
  168.2 0.0 copy-start.4
  168.2 9.9 %fusion.2 = f32[1024,512]{1,0:T(8,128)S(1)} fusion(bf16[1024,5120]{1,0:T(8,128)(2,1)} %all-gather.6.cloned.1.call-done, bf16[1,5120,512]{2,1,0:T(8,128)(2,1)} %param.12), kind=kOutput, calls=%fused_computation.2 | convolution fusion | flops 5368709120 | bytes 17825792 | tf_op jit(solution)/shard_map/dot_general | solution.py:46
  178.2 0.0 copy-done.4
  178.2 8.4 %multiply_convert_fusion = bf16[1024,512]{1,0:T(8,128)(2,1)} fusion(f32[1024,512]{1,0:T(8,128)S(1)} %fusion.2, bf16[1024,5120]{1,0:T(8,128)(2,1)S(1)} %copy-done.4, bf16[1,5120,512]{2,1,0:T(8,128)(2,1)} %param.11), kind=kOutput, calls=%fused_computation.8 | convolution fusion | flops 5371854848 | bytes 18874368 | tf_op jit(solution)/shard_map/dot_general | solution.py:45
  186.6 0.0 all-gather.8.cloned.1.call-update
  186.6 0.0 reduce-scatter.2.cloned.1.call-start
  186.7 33.2 %all-gather.8.cloned.1.call-done = bf16[1024,1024]{1,0:T(8,128)(2,1)} async-done(((bf16[1024,512]{1,0:T(8,128)(2,1)}), bf16[1024,1024]{1,0:T(8,128)(2,1)}) %all-gather.8.cloned.1.call-update) | async-done | bytes 2097168 | tf_op jit(solution)/shard_map/all_gather | solution.py:48
  219.9 10.9 %fusion = f32[1024,2560]{1,0:T(8,128)} fusion(bf16[1024,1024]{1,0:T(8,128)(2,1)} %all-gather.8.cloned.1.call-done, bf16[1,1024,2560]{2,1,0:T(8,128)(2,1)} %param.13), kind=kOutput, calls=%fused_computation | convolution fusion | flops 5368709120 | bytes 17825792 | tf_op jit(solution)/shard_map/dot_general | solution.py:50
  230.8 0.0 reduce-scatter.2.cloned.1.call-update
  230.8 84.6 %reduce-scatter.2.cloned.1.call-done = f32[256,2560]{1,0:T(8,128)} async-done(((f32[1024,2560]{1,0:T(8,128)}), f32[256,2560]{1,0:T(8,128)}) %reduce-scatter.2.cloned.1.call-update) | async-done | bytes 2621456 | tf_op jit(solution)/shard_map/reduce_scatter | solution.py:49
  315.4 1.9 convert_element_type.36
  317.3 35.6 %all_to_all.25 = bf16[4,64,2560]{2,1,0:T(8,128)(2,1)S(1)} all-to-all(bf16[4,64,2560]{2,1,0:T(8,128)(2,1)S(1)} %bitcast.33), channel_id=1, replica_groups=mesh['section'=4,'expert'=4,'tensor'=2] {'expert'}, dimensions={0} | all-to-all | bytes 2621440 | tf_op jit(solution)/shard_map/all_to_all | solution.py:55
  352.9 1.2 convolution_convert_fusion.1
  (3 shorter events, 0.0 us)
Async XLA Ops:
  6.5 7.3 %copy-start = (bf16[2560,4]{0,1:T(4,128)(2,1)S(1)}, bf16[2560,4]{0,1:T(4,128)(2,1)}, u32[]{:S(2)}) copy-start(bf16[2560,4]{0,1:T(4,128)(2,1)} %param.9) | copy-start | bytes 61444
  6.5 18.8 %copy-start.1 = (bf16[128,2560]{1,0:T(8,128)(2,1)S(1)}, bf16[128,2560]{1,0:T(8,128)(2,1)}, u32[]{:S(2)}) copy-start(bf16[128,2560]{1,0:T(8,128)(2,1)} %param.7) | copy-start | bytes 1966084
  6.5 18.8 %copy-start.2 = (f32[2560]{0:T(1024)S(1)}, f32[2560]{0:T(1024)}, u32[]{:S(2)}) copy-start(f32[2560]{0:T(1024)} %param.8) | copy-start | bytes 30724
  6.5 18.2 %copy-start.3 = (s32[128,1]{0,1:T(1,128)S(1)}, s32[128,1]{0,1:T(1,128)}, u32[]{:S(2)}) copy-start(s32[128,1]{0,1:T(1,128)} %param.10) | copy-start | bytes 1540
  6.5 89.9 %all-gather.4.cloned.1.call-start = ((), (), s32[]{:S(2)}) async-start(), calls=%async_computation.3 | async-start | bytes 3932160 | tf_op jit(solution)/shard_map/all_gather | solution.py:43
  59.2 109.0 %all-gather.6.cloned.1.call-start = ((), (), s32[]{:S(2)}) async-start(), calls=%async_computation.4 | async-start | bytes 13107200 | tf_op jit(solution)/shard_map/all_gather | solution.py:44
  96.5 123.4 %all-gather.8.cloned.1.call-start = ((), (), s32[]{:S(2)}) async-start(), calls=%async_computation.5 | async-start | bytes 3145728 | tf_op jit(solution)/shard_map/all_gather | solution.py:48
  168.2 10.0 %copy-start.4 = (bf16[1024,5120]{1,0:T(8,128)(2,1)S(1)}, bf16[1024,5120]{1,0:T(8,128)(2,1)}, u32[]{:S(2)}) copy-start(bf16[1024,5120]{1,0:T(8,128)(2,1)} %all-gather.6.cloned.1.call-done) | copy-start | bytes 31457284
  186.6 128.8 %reduce-scatter.2.cloned.1.call-start = ((), (), s32[]{:S(2)}) async-start(), calls=%async_computation.6 | async-start | bytes 13107200 | tf_op jit(solution)/shard_map/reduce_scatter | solution.py:49
Sparse Core Ops, SparseCore 0:
  59.3 37.1 all-gather.3
  98.0 70.1 all-gather.5
  186.8 33.0 all-gather.7
  231.0 84.3 reduce-scatter.1
where the time goes:
time: 361 us
  waiting for transfers between devices  227 us (63%)
  blocking collectives  83.9 us (23%)
  matrix products  32.7 us (9%)
  between operations  13.2 us (4%)
  other arithmetic  3.86 us (1%)
    reduce_scatter x1, waiting for transfers between devices, on_device(): lax.psum_scatter(jnp.dot(full_hidden, down_rows, preferred_element_type=j...  84.6 us
    all_gather x1, waiting for transfers between devices, on_device(): piece = lax.all_gather(widened, 'section', axis=0, tiled=True)  71.7 us
    all_gather x1, waiting for transfers between devices, on_device(): widened = lax.all_gather(arrived, 'tensor', axis=1, tiled=True)  37.2 us
    all_to_all x1, blocking collectives, on_device(): lax.all_to_all(summed.astype(jnp.bfloat16), 'expert', split_axis=0, conca...  35.6 us
    all_gather x1, waiting for transfers between devices, on_device(): full_hidden = lax.all_gather(hidden, 'tensor', axis=1, tiled=True)  33.2 us
    all_to_all x1, blocking collectives, on_device(): lax.all_to_all(outgoing, 'expert', split_axis=0, concat_axis=0, tiled=True)  33.1 us
    dot_general x1, matrix products, on_device(): jnp.dot(full_hidden, down_rows, preferred_element_type=jnp.float32)  10.9 us
    dot_general x1, matrix products, on_device(): upper = jnp.dot(piece, up_cols, preferred_element_type=jnp.float32)  9.94 us
  transfers between devices with their start and end apart: 4, of which 4 were waited for; matrix products, arithmetic and copies ran while one was open for 0% of the time, Pallas kernels for 0%

commit v1 on v0

--- a/solution.py
+++ b/solution.py
@@ -1,3 +1,4 @@
+import functools
 import jax
 import jax.numpy as jnp
 from jax import lax
@@ -5,6 +6,25 @@
 
 D = 5120
 EPSILON = 1e-05
+
+
+def convert_arrays(matrix, device_axis):
+    many = jax.lax.axis_size(device_axis)
+    block_list = [matrix]
+    for s in tuple(range(many - 1)):
+        block_list.append(
+            jax.lax.ppermute(
+                block_list[-1], device_axis, [(ix, (ix + 1) % many) for ix in range(many)]
+            )
+        )
+    return jnp.roll(
+        jnp.concatenate(block_list[::-1], 0),
+        (jax.lax.axis_index(device_axis) + 1) * matrix.shape[0],
+        0,
+    )
+
+
+follow_positions = functools.partial(convert_arrays, device_axis="section")
 
 
 def slot_table(expert_ids, experts, capacity):
@@ -41,7 +61,7 @@
     up_cols = up_proj[0]
     down_rows = down_proj[0]
     widened = lax.all_gather(arrived, "tensor", axis=1, tiled=True)
-    piece = lax.all_gather(widened, "section", axis=0, tiled=True)
+    piece = follow_positions(widened)
     gate = jnp.dot(piece, gate_cols, preferred_element_type=jnp.float32)
     upper = jnp.dot(piece, up_cols, preferred_element_type=jnp.float32)
     hidden = (jax.nn.silu(gate) * upper).astype(jnp.bfloat16)

time: 361 us -> 393 us (1.089)
  waiting for transfers between devices: 227 us -> 249 us
  local copies, waits for them, and re-layouts: 0.02 us -> 11.1 us
    ppermute x0 -> x3, waiting for transfers between devices: none -> 93.9 us  [convert_arrays(): jax.lax.ppermute(block_list[-1], device_axis, [(ix, (ix + 1) % many) for...]
    all_gather x1 -> x0, waiting for transfers between devices: 71.7 us -> none  [on_device(): piece = lax.all_gather(widened, 'section', axis=0, tiled=True)]
    unnamed x10 -> x19, local copies, waits for them, and re-layouts: 0.02 us -> 11 us
  transfers between devices with their start and end apart: 4 -> 6, of which waited for: 4 -> 6; matrix products, arithmetic and copies ran while one was open for 0% -> 0% of each run, Pallas kernels for 0% -> 0%
where the time goes in v1:
time: 393 us
  waiting for transfers between devices  249 us (63%)
  blocking collectives  83.9 us (21%)
  matrix products  29 us (7%)
  between operations  13.2 us (3%)
  local copies, waits for them, and re-layouts  11.1 us (3%)
  other arithmetic  6.49 us (2%)
    ppermute x3, waiting for transfers between devices, convert_arrays(): jax.lax.ppermute(block_list[-1], device_axis, [(ix, (ix + 1) % many) for...  93.9 us
    reduce_scatter x1, waiting for transfers between devices, on_device(): lax.psum_scatter(jnp.dot(full_hidden, down_rows, preferred_element_type=j...  84.6 us
    all_gather x1, waiting for transfers between devices, on_device(): widened = lax.all_gather(arrived, 'tensor', axis=1, tiled=True)  37.3 us
    all_to_all x1, blocking collectives, on_device(): lax.all_to_all(summed.astype(jnp.bfloat16), 'expert', split_axis=0, conca...  35.6 us
    all_gather x1, waiting for transfers between devices, on_device(): full_hidden = lax.all_gather(hidden, 'tensor', axis=1, tiled=True)  33.2 us
    all_to_all x1, blocking collectives, on_device(): lax.all_to_all(outgoing, 'expert', split_axis=0, concat_axis=0, tiled=True)  33.1 us
    unnamed x19, local copies, waits for them, and re-layouts  11 us
    dot_general x1, matrix products, on_device(): jnp.dot(full_hidden, down_rows, preferred_element_type=jnp.float32)  10.9 us
  transfers between devices with their start and end apart: 6, of which 6 were waited for; matrix products, arithmetic and copies ran while one was open for 0% of the time, Pallas kernels for 0%

profile of v1, /device:TPU:0, one launch (start us, length us, event | category | flops | bytes accessed | tf_op | source)
XLA Modules:
  0.0 392.8 jit_solution(3552048680546404500)
XLA Ops:
  6.5 0.0 copy-start
  6.5 0.0 all-gather.3.cloned.1.call-start
  6.5 0.8 fusion.17
  7.4 0.2 reduce_window_sum.11
  7.5 0.8 select_reduce_fusion.1
  8.4 0.7 fusion.18
  9.0 1.3 fusion.8
  10.3 5.9 %psum.14 = f32[128,1]{0,1:T(1,128)S(1)} all-reduce(f32[128,1]{0,1:T(1,128)S(1)} %bitcast.35), channel_id=1, replica_groups=mesh['section'=4,'expert'=4,'tensor'=2] {'tensor'}, use_global_device_ids=true, to_apply=%region_3.0 | all-reduce | flops 128 | bytes 1024 | tf_op jit(solution)/shard_map/psum | solution.py:49
  16.2 0.0 copy-done
  16.2 1.5 fusion.12
  17.7 9.4 %psum.15 = f32[128,4]{1,0:T(8,128)S(1)} all-reduce(f32[128,4]{1,0:T(8,128)S(1)} %fusion.12), channel_id=1, replica_groups=mesh['section'=4,'expert'=4,'tensor'=2] {'tensor'}, use_global_device_ids=true, to_apply=%region_4.5 | all-reduce | flops 512 | bytes 4096 | tf_op jit(solution)/shard_map/psum | solution.py:51
  27.1 0.8 select_reduce_fusion
  27.9 0.0 copy-done.3
  27.9 1.3 convolution_convert_fusion
  29.3 33.1 %all_to_all.24 = bf16[4,64,2560]{2,1,0:T(8,128)(2,1)} all-to-all(bf16[4,64,2560]{2,1,0:T(8,128)(2,1)S(1)} %bitcast.29), channel_id=1, replica_groups=mesh['section'=4,'expert'=4,'tensor'=2] {'expert'}, dimensions={0} | all-to-all | bytes 2621440 | tf_op jit(solution)/shard_map/all_to_all | solution.py:59
  62.4 0.0 all-gather.3.cloned.1.call-update
  62.4 0.0 all-gather.5.cloned.1.call-start
  62.5 37.3 %all-gather.3.cloned.1.call-done = bf16[256,5120]{1,0:T(8,128)(2,1)} async-done(((bf16[256,2560]{1,0:T(8,128)(2,1)}), bf16[256,5120]{1,0:T(8,128)(2,1)}) %all-gather.3.cloned.1.call-update) | async-done | bytes 2621456 | tf_op jit(solution)/shard_map/all_gather | solution.py:63
  99.7 0.0 collective-permute-start
  99.7 31.3 %collective-permute-done = bf16[256,5120]{1,0:T(8,128)(2,1)S(1)} collective-permute-done((bf16[256,5120]{1,0:T(8,128)(2,1)}, bf16[256,5120]{1,0:T(8,128)(2,1)S(1)}, u32[]{:S(2)}, u32[]{:S(2)}) %collective-permute-start) | collective-permute-done | bytes 2621472 | tf_op jit(solution)/shard_map/ppermute | solution.py:16
  131.0 0.0 collective-permute-start.1
  131.0 31.2 %collective-permute-done.1 = bf16[256,5120]{1,0:T(8,128)(2,1)} collective-permute-done((bf16[256,5120]{1,0:T(8,128)(2,1)S(1)}, bf16[256,5120]{1,0:T(8,128)(2,1)}, u32[]{:S(2)}, u32[]{:S(2)}) %collective-permute-start.1) | collective-permute-done | bytes 2621472 | tf_op jit(solution)/shard_map/ppermute | solution.py:16
  162.2 0.0 collective-permute-start.2
  162.2 31.4 %collective-permute-done.2 = bf16[256,5120]{1,0:T(8,128)(2,1)} collective-permute-done((bf16[256,5120]{1,0:T(8,128)(2,1)}, bf16[256,5120]{1,0:T(8,128)(2,1)}, u32[]{:S(2)}, u32[]{:S(2)}) %collective-permute-start.2) | collective-permute-done | bytes 2621472 | tf_op jit(solution)/shard_map/ppermute | solution.py:16
  193.6 1.9 constant_dynamic-update-slice_fusion.7
  195.5 1.9 constant_dynamic-update-slice_fusion.6
  197.4 0.2 constant_dynamic-update-slice_fusion.5
  197.6 1.6 copy-done.2
  199.1 0.2 constant_dynamic-update-slice_fusion.4
  199.3 1.9 constant_dynamic-update-slice_fusion.3
  201.2 0.0 slice-start
  201.2 2.1 constant_dynamic-update-slice_fusion.2
  203.3 0.0 slice-start.1
  203.3 0.2 constant_dynamic-update-slice_fusion.1
  203.5 0.2 constant_dynamic-update-slice_fusion
  203.7 0.5 slice-done
  204.2 0.6 slice-done.1
  204.8 5.6 %fusion.2 = f32[1024,512]{1,0:T(8,128)S(1)} fusion(bf16[2048,5120]{1,0:T(8,128)(2,1)S(1)} %constant_dynamic-update-slice_fusion, s32[]{:T(128)S(6)} %select_n.19, bf16[1,5120,512]{2,1,0:T(8,128)(2,1)S(1)} %bitcast.37), kind=kOutput, calls=%fused_computation.2 | convolution fusion | flops 5368709120 | bytes 17825796 | tf_op jit(solution)/shard_map/dot_general | solution.py:65
  210.3 8.5 %multiply_convert_fusion = bf16[1024,512]{1,0:T(8,128)(2,1)} fusion(f32[1024,512]{1,0:T(8,128)S(1)} %fusion.2, bf16[1,5120,512]{2,1,0:T(8,128)(2,1)} %param.12, bf16[2048,5120]{1,0:T(8,128)(2,1)S(1)} %constant_dynamic-update-slice_fusion, s32[]{:T(128)S(6)} %select_n.19), kind=kOutput, calls=%fused_computation.10 | convolution fusion | flops 5371854848 | bytes 18874372 | tf_op jit(solution)/shard_map/dot_general | solution.py:66
  218.8 0.0 all-gather.5.cloned.1.call-update
  218.8 0.0 reduce-scatter.2.cloned.1.call-start
  218.9 33.2 %all-gather.5.cloned.1.call-done = bf16[1024,1024]{1,0:T(8,128)(2,1)} async-done(((bf16[1024,512]{1,0:T(8,128)(2,1)}), bf16[1024,1024]{1,0:T(8,128)(2,1)}) %all-gather.5.cloned.1.call-update) | async-done | bytes 2097168 | tf_op jit(solution)/shard_map/all_gather | solution.py:68
  252.1 10.9 %fusion.4 = f32[1024,2560]{1,0:T(8,128)} fusion(bf16[1024,1024]{1,0:T(8,128)(2,1)} %all-gather.5.cloned.1.call-done, bf16[1,1024,2560]{2,1,0:T(8,128)(2,1)} %param.13), kind=kOutput, calls=%fused_computation.4 | convolution fusion | flops 5368709120 | bytes 17825792 | tf_op jit(solution)/shard_map/dot_general | solution.py:70
  263.0 0.0 reduce-scatter.2.cloned.1.call-update
  263.0 84.6 %reduce-scatter.2.cloned.1.call-done = f32[256,2560]{1,0:T(8,128)} async-done(((f32[1024,2560]{1,0:T(8,128)}), f32[256,2560]{1,0:T(8,128)}) %reduce-scatter.2.cloned.1.call-update) | async-done | bytes 2621456 | tf_op jit(solution)/shard_map/reduce_scatter | solution.py:69
  347.6 1.9 convert_element_type.36
  349.5 35.6 %all_to_all.25 = bf16[4,64,2560]{2,1,0:T(8,128)(2,1)S(1)} all-to-all(bf16[4,64,2560]{2,1,0:T(8,128)(2,1)S(1)} %bitcast.31), channel_id=1, replica_groups=mesh['section'=4,'expert'=4,'tensor'=2] {'expert'}, dimensions={0} | all-to-all | bytes 2621440 | tf_op jit(solution)/shard_map/all_to_all | solution.py:75
  385.0 1.2 convolution_convert_fusion.1
  (7 shorter events, 0.0 us)
Async XLA Ops:
  6.5 9.7 %copy-start = (bf16[2560,4]{0,1:T(4,128)(2,1)S(1)}, bf16[2560,4]{0,1:T(4,128)(2,1)}, u32[]{:S(2)}) copy-start(bf16[2560,4]{0,1:T(4,128)(2,1)} %param.9) | copy-start | bytes 61444
  6.5 21.4 %copy-start.3 = (bf16[128,2560]{1,0:T(8,128)(2,1)S(1)}, bf16[128,2560]{1,0:T(8,128)(2,1)}, u32[]{:S(2)}) copy-start(bf16[128,2560]{1,0:T(8,128)(2,1)} %param.7) | copy-start | bytes 1966084
  6.5 93.2 %all-gather.3.cloned.1.call-start = ((), (), s32[]{:S(2)}) async-start(), calls=%async_computation.3 | async-start | bytes 3932160 | tf_op jit(solution)/shard_map/all_gather | solution.py:63
  62.4 189.7 %all-gather.5.cloned.1.call-start = ((), (), s32[]{:S(2)}) async-start(), calls=%async_computation.4 | async-start | bytes 3145728 | tf_op jit(solution)/shard_map/all_gather | solution.py:68
  99.7 31.3 %collective-permute-start = (bf16[256,5120]{1,0:T(8,128)(2,1)}, bf16[256,5120]{1,0:T(8,128)(2,1)S(1)}, u32[]{:S(2)}, u32[]{:S(2)}) collective-permute-start(bf16[256,5120]{1,0:T(8,128)(2,1)} %all-gather.3.cloned.1.call-done), channel_id=1, source_target_pairs={{0,8},{8,16},{16,24},{24,0},{1,9},{9,17},{17,25},{25,1},{2,10},{10... | collective-permute-start | bytes 7864328 | tf_op jit(solution)/shard_map/ppermute | solution.py:16
  131.0 31.2 %collective-permute-start.1 = (bf16[256,5120]{1,0:T(8,128)(2,1)S(1)}, bf16[256,5120]{1,0:T(8,128)(2,1)}, u32[]{:S(2)}, u32[]{:S(2)}) collective-permute-start(bf16[256,5120]{1,0:T(8,128)(2,1)S(1)} %collective-permute-done), channel_id=1, source_target_pairs={{0,8},{8,16},{16,24},{24,0},{1,9},{9,17},{17,25},{25,1},{2,10},{10... | collective-permute-start | bytes 7864328 | tf_op jit(solution)/shard_map/ppermute | solution.py:16
  162.2 31.4 %collective-permute-start.2 = (bf16[256,5120]{1,0:T(8,128)(2,1)}, bf16[256,5120]{1,0:T(8,128)(2,1)}, u32[]{:S(2)}, u32[]{:S(2)}) collective-permute-start(bf16[256,5120]{1,0:T(8,128)(2,1)} %collective-permute-done.1), channel_id=1, source_target_pairs={{0,8},{8,16},{16,24},{24,0},{1,9},{9,17},{17,25},{25,1},{2,10},{10... | collective-permute-start | bytes 7864328 | tf_op jit(solution)/shard_map/ppermute | solution.py:16
  197.4 1.7 copy-start.2
  201.2 3.0 slice-start
  203.3 1.5 slice-start.1
  218.8 128.8 %reduce-scatter.2.cloned.1.call-start = ((), (), s32[]{:S(2)}) async-start(), calls=%async_computation.5 | async-start | bytes 13107200 | tf_op jit(solution)/shard_map/reduce_scatter | solution.py:69
  347.6 38.7 %copy-start.1 = (bf16[2560,4]{0,1:T(4,128)(2,1)S(1)}, bf16[2560,4]{0,1:T(4,128)(2,1)}, u32[]{:S(2)}) copy-start(bf16[2560,4]{0,1:T(4,128)(2,1)} %param.9) | copy-start | bytes 61444
Sparse Core Ops, SparseCore 0:
  62.5 37.1 all-gather.2
  218.9 33.0 all-gather.4
  263.2 84.3 reduce-scatter.1
